TPU v7x, 128 devices: a whole 4x4x4 slice. The times are simulated.
128 devices in a mesh: fsdp: 32 (over z, x, core), tensor: 4 (over y).
Axes of the slice: x: 4, y: 4, z: 4, core: 2. Of those that a mesh axis runs over, the one named last changes fastest.
Arguments:
- hidden: bfloat16 [512, 28672], P('tensor', 'fsdp'), may hold values from -6 to 6
- down_weight: bfloat16 [28672, 16384], P('fsdp', 'tensor'), may hold values from -0.03125 to 0.03125
- covariance: float32 [16384, 16384], P('tensor', 'fsdp'), as said below
- keep_index: int32 [32, 8], P('fsdp'), may hold values from -1 to 15, as said below
- start_basis: float32 [16384, 512], P('fsdp'), may hold values from -6 to 6
Outputs:
- mlp_out: bfloat16 [512, 16384], P('fsdp', 'tensor')
- new_covariance: float32 [16384, 16384], P('tensor', 'fsdp')
- first_basis: float32 [16384, 512], P(('tensor', 'fsdp'))
- final_basis: float32 [16384, 512], P('fsdp')
Inputs may be any that keep to these rules, and one draw needn't show every extreme that they name: `keep_index`: row b lists first between 1 and 8 distinct positions of 0 to 15, then -1 in the remaining slots; in every draw some row lists 8 positions. covariance is exactly symmetric and positive definite.
All inputs are finite; a program needn't handle non-finite values.
Results may differ from a plain program's by a relative error of at most 0.0015.
Values may be sent and summed in bfloat16 or wider, within the bound.
A program may use at most 128 MiB of HBM per device.

v0:
```python
import math
import jax
import jax.numpy as jnp
from jax import lax
from jax.sharding import PartitionSpec as P

D = 16384
TOK_DEV = 16


def broadcast(x, axis, root):
    mine = lax.axis_index(axis) == root
    return lax.psum(jnp.where(mine, x, jnp.zeros_like(x)), axis)


def gram_local(image_rows):
    return jnp.dot(
        image_rows.T,
        image_rows,
        precision=lax.Precision.HIGHEST,
        preferred_element_type=jnp.float32,
    )


def solve_rows(image_rows, lower_factor):
    return jax.scipy.linalg.solve_triangular(lower_factor, image_rows.T, lower=True).T


def body(hidden, down_weight, covariance, keep_index, start_basis):
    highest = lax.Precision.HIGHEST
    fsdp_count = lax.axis_size("fsdp")
    total_tokens = TOK_DEV * fsdp_count
    quarter = covariance.shape[0]
    block_width = covariance.shape[1]
    share_rows = quarter // fsdp_count
    group_size = fsdp_count // lax.axis_size("tensor")
    all_hidden = lax.all_gather(hidden, "tensor", axis=0, tiled=True)
    mlp_out = lax.psum_scatter(
        jnp.dot(all_hidden, down_weight, preferred_element_type=jnp.float32),
        "fsdp",
        scatter_dimension=0,
        tiled=True,
    ).astype(jnp.bfloat16)
    listed = keep_index[0]
    fsdp_index = lax.axis_index("fsdp")
    col_offset = fsdp_index % group_size * block_width
    source_index = fsdp_index // group_size
    positions = jnp.arange(mlp_out.shape[0], dtype=jnp.int32)
    marked = jnp.any(listed[:, None] == positions[None, :], axis=0).astype(jnp.bfloat16)
    row_data = lax.all_gather(mlp_out * marked[:, None], "fsdp", axis=0, tiled=True)
    column_data = broadcast(
        lax.dynamic_slice_in_dim(row_data, col_offset, block_width, 1), "tensor", source_index
    )
    update = lax.dot_general(
        row_data, column_data, (((0,), (0,)), ((), ())), preferred_element_type=jnp.float32
    )
    new_covariance = covariance + update * (1.0 / total_tokens)
    partial_image = jnp.dot(
        new_covariance, start_basis, precision=highest, preferred_element_type=jnp.float32
    )
    first_image = lax.psum(partial_image, "fsdp")
    first_gram = lax.psum(gram_local(first_image), "tensor")
    own_image = lax.dynamic_slice_in_dim(first_image, fsdp_index * share_rows, share_rows, 0)
    first_factor = jnp.linalg.cholesky(first_gram)
    first_basis = solve_rows(own_image, first_factor) * math.sqrt(D)
    carried = solve_rows(first_image, first_factor)
    partial_second = lax.dot_general(
        new_covariance,
        carried,
        (((0,), (0,)), ((), ())),
        precision=highest,
        preferred_element_type=jnp.float32,
    )
    second = lax.psum(partial_second, "tensor")
    second_gram = lax.psum(gram_local(second), "fsdp")
    final_basis = solve_rows(second, jnp.linalg.cholesky(second_gram)) * math.sqrt(D)
    return (mlp_out, new_covariance, first_basis, final_basis)


def solution(mesh):
    placed = (
        P("tensor", "fsdp"),
        P("fsdp", "tensor"),
        P("tensor", "fsdp"),
        P("fsdp", None),
        P("fsdp", None),
    )
    return jax.shard_map(
        body,
        mesh=mesh,
        in_specs=placed,
        out_specs=(
            P("fsdp", "tensor"),
            P("tensor", "fsdp"),
            P(("tensor", "fsdp"), None),
            P("fsdp", None),
        ),
        check_vma=False,
    )
```

profile of v0, /device:TPU:1, one launch (start us, length us, event | category | flops | bytes accessed | tf_op | source)
XLA Modules:
  0.0 948.6 jit_solution(741812926708005223)
XLA Ops:
  7.2 14.1 %all_gather.6 = bf16[512,896]{1,0:T(8,128)(2,1)S(1)} all-gather(bf16[128,896]{1,0:T(8,128)(2,1)} %param.6), channel_id=1, replica_groups=mesh['fsdp'=32,'tensor'=4] {'tensor'}, dimensions={0}, use_global_device_ids=true | all-gather | bytes 1146880 | tf_op jit(solution)/shard_map/all_gather | solution.py:37
  31.8 94.6 %reduce-scatter.2.cloned.1.call-done = f32[16,4096]{1,0:T(8,128)} async-done(((f32[512,4096]{1,0:T(8,128)}), f32[16,4096]{1,0:T(8,128)}) %reduce-scatter.2.cloned.1.call-update) | async-done | bytes 262160 | tf_op jit(solution)/shard_map/reduce_scatter | solution.py:38
  128.2 48.6 %all-gather.2.cloned.1.call-done = bf16[512,4096]{1,0:T(8,128)(2,1)} async-done(((bf16[16,4096]{1,0:T(8,128)(2,1)}), bf16[512,4096]{1,0:T(8,128)(2,1)}) %all-gather.2.cloned.1.call-update) | async-done | bytes 4194320 | tf_op jit(solution)/shard_map/all_gather | solution.py:50
  178.8 40.7 %all-reduce.7.cloned.1.call-done = bf16[512,512]{1,0:T(8,128)(2,1)} async-done(((bf16[512,512]{1,0:T(8,128)(2,1)}), bf16[512,512]{1,0:T(8,128)(2,1)}) %all-reduce.7.cloned.1.call-update) | async-done | bytes 524304 | tf_op jit(solution)/shard_map/psum | solution.py:13
  230.3 15.7 %fusion.97 = f32[4096,512]{1,0:T(8,128)} fusion(f32[4096,512]{1,0:T(8,128)S(1)} %multiply_add_fusion, f32[512,512]{1,0:T(8,128)S(1)} %copy-done), kind=kOutput, calls=%fused_computation.170 | convolution fusion | flops 12884901888 | bytes 17825792 | tf_op jit(solution)/shard_map/dot_general | solution.py:58
  246.4 122.9 %all-reduce.9.cloned.1.call-done = f32[4096,512]{1,0:T(8,128)} async-done(((f32[4096,512]{1,0:T(8,128)}), f32[4096,512]{1,0:T(8,128)}) %all-reduce.9.cloned.1.call-update) | async-done | bytes 8388624 | tf_op jit(solution)/shard_map/psum | solution.py:61
  369.2 18.5 %fusion.98 = f32[512,512]{0,1:T(8,128)} fusion(f32[4096,512]{1,0:T(8,128)} %all-reduce.9.cloned.1.call-done), kind=kOutput, calls=%fused_computation.171 | convolution fusion | flops 12884901888 | bytes 9437184 | tf_op jit(solution)/shard_map/dot_general | solution.py:17
  388.8 43.1 %all-reduce.11.cloned.1.call-done = f32[512,512]{0,1:T(8,128)} async-done(((f32[512,512]{0,1:T(8,128)}), f32[512,512]{0,1:T(8,128)}) %all-reduce.11.cloned.1.call-update) | async-done | bytes 1048592 | tf_op jit(solution)/shard_map/psum | solution.py:62
  434.9 11.7 %cholesky.286 = f32[128,128]{1,0:T(8,128)S(1)} custom-call(f32[128,128]{1,0:T(8,128)S(1)} %cholesky.426), custom_call_target="Cholesky" | custom-call | tf_op jit(solution)/shard_map/jit(cholesky)/cholesky | solution.py:64
  457.3 11.7 %cholesky.305 = f32[128,128]{1,0:T(8,128)S(1)} custom-call(f32[128,128]{1,0:T(8,128)S(1)} %cholesky.430), custom_call_target="Cholesky" | custom-call | tf_op jit(solution)/shard_map/jit(cholesky)/cholesky | solution.py:64
  469.0 18.5 %custom-call.37 = f32[1,128,128]{1,2,0:T(8,128)S(1)} custom-call(f32[1,128,128]{2,1,0:T(8,128)S(1)} %get-tuple-element.67), custom_call_target="InvertDiagBlocksLowerTriangular" | custom-call | tf_op jit(solution)/shard_map/jit(cholesky)/cholesky | solution.py:64
  488.2 11.7 %cholesky.326 = f32[128,128]{1,0:T(8,128)S(1)} custom-call(f32[128,128]{1,0:T(8,128)S(1)} %cholesky.435), custom_call_target="Cholesky" | custom-call | tf_op jit(solution)/shard_map/jit(cholesky)/cholesky | solution.py:64
  510.4 11.7 %cholesky.343 = f32[128,128]{1,0:T(8,128)S(1)} custom-call(f32[128,128]{1,0:T(8,128)S(1)} %convolution_subtract_fusion.13), custom_call_target="Cholesky" | custom-call | tf_op jit(solution)/shard_map/jit(cholesky)/cholesky | solution.py:64
  535.1 39.3 %custom-call.31 = f32[4,128,128]{1,2,0:T(8,128)S(1)} custom-call(f32[4,128,128]{2,1,0:T(8,128)S(1)} %get-tuple-element.12), custom_call_target="InvertDiagBlocksLowerTriangular" | custom-call | tf_op jit(solution)/shard_map/jit(_solve_triangular)/triangular_solve | solution.py:26
  595.9 12.4 %fusion.14 = f32[128,4096]{0,1:T(8,128)S(1)} fusion(f32[128,4096]{1,0:T(8,128)S(1)} %fusion.80, f32[128,4096]{1,0:T(8,128)S(1)} %fusion.78, f32[128,4096]{1,0:T(8,128)S(1)} %fusion.20, f32[512,4096]{0,1:T(8,128)} %bitcast.127, f32[512,512]{1,0:T(8,128)S(1)} %get-tuple-element.179), kind=kOutput, calls=%fused_computation.21 | convolution fusion | flops 2419589120 | bytes 10682368 | tf_op jit(solution)/shard_map/jit(_solve_triangular)/triangular_solve | solution.py:26
  610.3 29.5 %fusion = f32[512,512]{1,0:T(8,128)} fusion(f32[4096,512]{1,0:T(8,128)S(1)} %bitcast.129, f32[128,4096]{1,0:T(8,128)S(1)} %fusion.82, f32[128,4096]{1,0:T(8,128)S(1)} %fusion.80, f32[128,4096]{1,0:T(8,128)S(1)} %fusion.78, f32[128,4096]{1,0:T(8,128)S(1)} %fusion.20), kind=kOutput, calls=%fused_computation.4 | convolution fusion | flops 12891193344 | bytes 17825792 | tf_op jit(solution)/shard_map/dot_general | solution.py:67
  641.5 45.5 %all-reduce.13.cloned.1.call-done = f32[512,512]{1,0:T(8,128)} async-done(((f32[512,512]{1,0:T(8,128)}), f32[512,512]{1,0:T(8,128)}) %all-reduce.13.cloned.1.call-update) | async-done | bytes 1048592 | tf_op jit(solution)/shard_map/psum | solution.py:74
  693.1 106.8 %all-reduce.15.cloned.1.call-done = f32[512,512]{0,1:T(8,128)} async-done(((f32[512,512]{0,1:T(8,128)}), f32[512,512]{0,1:T(8,128)}) %all-reduce.15.cloned.1.call-update) | async-done | bytes 1048592 | tf_op jit(solution)/shard_map/psum | solution.py:75
  802.9 11.7 %cholesky.358 = f32[128,128]{1,0:T(8,128)S(1)} custom-call(f32[128,128]{1,0:T(8,128)S(1)} %cholesky.439), custom_call_target="Cholesky" | custom-call | tf_op jit(solution)/shard_map/jit(cholesky)/cholesky | solution.py:76
  825.3 11.9 %cholesky.377 = f32[128,128]{1,0:T(8,128)S(1)} custom-call(f32[128,128]{1,0:T(8,128)S(1)} %cholesky.443), custom_call_target="Cholesky" | custom-call | tf_op jit(solution)/shard_map/jit(cholesky)/cholesky | solution.py:76
  837.2 9.8 %custom-call.40 = f32[1,128,128]{1,2,0:T(8,128)S(1)} custom-call(f32[1,128,128]{2,1,0:T(8,128)S(1)} %get-tuple-element.57), custom_call_target="InvertDiagBlocksLowerTriangular" | custom-call | tf_op jit(solution)/shard_map/jit(cholesky)/cholesky | solution.py:76
  847.7 11.7 %cholesky.398 = f32[128,128]{1,0:T(8,128)S(1)} custom-call(f32[128,128]{1,0:T(8,128)S(1)} %cholesky.448), custom_call_target="Cholesky" | custom-call | tf_op jit(solution)/shard_map/jit(cholesky)/cholesky | solution.py:76
  869.9 11.9 %cholesky.415 = f32[128,128]{1,0:T(8,128)S(1)} custom-call(f32[128,128]{1,0:T(8,128)S(1)} %convolution_subtract_fusion.11), custom_call_target="Cholesky" | custom-call | tf_op jit(solution)/shard_map/jit(cholesky)/cholesky | solution.py:76
  895.7 39.3 %custom-call.32 = f32[4,128,128]{1,2,0:T(8,128)S(1)} custom-call(f32[4,128,128]{2,1,0:T(8,128)S(1)} %get-tuple-element.20), custom_call_target="InvertDiagBlocksLowerTriangular" | custom-call | tf_op jit(solution)/shard_map/jit(_solve_triangular)/triangular_solve | solution.py:26
  (136 shorter events, 151.3 us)
Async XLA Ops:
  7.2 223.2 %copy-start = (f32[512,512]{1,0:T(8,128)S(1)}, f32[512,512]{1,0:T(8,128)}, u32[]{:S(2)}) copy-start(f32[512,512]{1,0:T(8,128)} %param.10) | copy-start | bytes 3145732
  7.2 119.2 %reduce-scatter.2.cloned.1.call-start = ((), (), s32[]{:S(2)}) async-start(), calls=%async_computation.1 | async-start | bytes 8650752 | tf_op jit(solution)/shard_map/reduce_scatter | solution.py:38
  31.1 0.7 copy-start.4
  31.1 145.6 %all-gather.2.cloned.1.call-start = ((), (), s32[]{:S(2)}) async-start(), calls=%async_computation.2 | async-start | bytes 4325376 | tf_op jit(solution)/shard_map/all_gather | solution.py:50
  128.1 91.4 %all-reduce.7.cloned.1.call-start = ((), (), s32[]{:S(2)}) async-start(), calls=%async_computation.3 | async-start | bytes 1048576 | tf_op jit(solution)/shard_map/psum | solution.py:13
  178.7 190.5 %all-reduce.9.cloned.1.call-start = ((), (), s32[]{:S(2)}) async-start(), calls=%async_computation.4 | async-start | bytes 16777216 | tf_op jit(solution)/shard_map/psum | solution.py:61
  226.9 3.4 copy-start.2
  246.1 185.8 %all-reduce.11.cloned.1.call-start = ((), (), s32[]{:S(2)}) async-start(), calls=%async_computation.5 | async-start | bytes 2097152 | tf_op jit(solution)/shard_map/psum | solution.py:62
  387.7 299.3 %all-reduce.13.cloned.1.call-start = ((), (), s32[]{:S(2)}) async-start(), calls=%async_computation.6 | async-start | bytes 2097152 | tf_op jit(solution)/shard_map/psum | solution.py:74
  593.9 16.4 %slice-start = ((s8[8388608]{0:T(1024)(128)(4,1)}), s8[4194304]{0:T(1024)(128)(4,1)S(1)}, s32[]{:S(2)}) async-start(s8[8388608]{0:T(1024)(128)(4,1)} %bitcast.128), calls=%async_computation.8 | async-start | bytes 8388608
  595.9 14.4 %slice-start.1 = ((s8[8388608]{0:T(1024)(128)(4,1)}), s8[4194304]{0:T(1024)(128)(4,1)S(1)}, s32[]{:S(2)}) async-start(s8[8388608]{0:T(1024)(128)(4,1)} %bitcast.128), calls=%async_computation.9 | async-start | bytes 8388608
  639.9 160.0 %all-reduce.15.cloned.1.call-start = ((), (), s32[]{:S(2)}) async-start(), calls=%async_computation.7 | async-start | bytes 2097152 | tf_op jit(solution)/shard_map/psum | solution.py:75
  802.9 132.1 %copy-start.3 = (f32[512,512]{1,0:T(8,128)S(1)}, f32[512,512]{1,0:T(8,128)}, u32[]{:S(2)}) copy-start(f32[512,512]{1,0:T(8,128)} %all-reduce.13.cloned.1.call-done) | copy-start | bytes 3145732
  935.5 5.8 copy-start.1
Sparse Core Ops, SparseCore 0:
  31.2 95.1 reduce-scatter.1
  129.2 47.4 all-gather.1
  179.7 39.7 all-reduce.6
  246.2 122.9 all-reduce.8
  387.9 43.9 all-reduce.10
  640.0 46.9 all-reduce.12
  691.5 108.3 all-reduce.14
where the time goes:
time: 957 us; the launch traced here: 949 us
  waiting for transfers between devices  502 us (52%)
  other arithmetic  253 us (26%)
  matrix products  132 us (14%)
  local copies, waits for them, and re-layouts  26.9 us (3%)
  between operations  20.2 us (2%)
  blocking collectives  14.1 us (1%)
    psum x1, waiting for transfers between devices, body(): first_image = lax.psum(partial_image, 'fsdp')  123 us
    psum x1, waiting for transfers between devices, body(): second_gram = lax.psum(gram_local(second), 'fsdp')  107 us
    reduce_scatter x1, waiting for transfers between devices, body(): lax.psum_scatter(jnp.dot(all_hidden, down_weight, preferred_element_type=...  94.6 us
    another operation x14, other arithmetic, body(): first_factor = jnp.linalg.cholesky(first_gram)  87 us
    another operation x15, other arithmetic, body(): jnp.linalg.cholesky(second_gram)  79.5 us
    another operation x5, other arithmetic, solve_rows(): jax.scipy.linalg.solve_triangular(lower_factor, image_rows.T, lower=True)  79.3 us
    all_gather x1, waiting for transfers between devices, body(): lax.all_gather(mlp_out * marked[:, None], 'fsdp', axis=0, tiled=True)  48.6 us
    psum x1, waiting for transfers between devices, body(): second = lax.psum(partial_second, 'tensor')  45.5 us
  transfers between devices with their start and end apart: 7, of which 7 were waited for; matrix products, arithmetic and copies ran while one was open for 0% of the time, Pallas kernels for 0%

commit v1 on v0

--- a/solution.py
+++ b/solution.py
@@ -47,7 +47,12 @@
     source_index = fsdp_index // group_size
     positions = jnp.arange(mlp_out.shape[0], dtype=jnp.int32)
     marked = jnp.any(listed[:, None] == positions[None, :], axis=0).astype(jnp.bfloat16)
-    row_data = lax.all_gather(mlp_out * marked[:, None], "fsdp", axis=0, tiled=True)
+    row_data = jnp.concatenate(
+        lax.all_to_all(
+            jnp.stack([mlp_out * marked[:, None]] * lax.axis_size("fsdp")), "fsdp", 0, 0
+        ),
+        axis=0,
+    )
     column_data = broadcast(
         lax.dynamic_slice_in_dim(row_data, col_offset, block_width, 1), "tensor", source_index
     )

time: 957 us -> 955 us (level)
    all_to_all x0 -> x1, waiting for transfers between devices: none -> 50.6 us  [body(): lax.all_to_all(jnp.stack([mlp_out * marked[:, None]] * lax.axis_size('fsd...]
    all_gather x1 -> x0, waiting for transfers between devices: 48.6 us -> none  [body(): lax.all_gather(mlp_out * marked[:, None], 'fsdp', axis=0, tiled=True)]
where the time goes in v1:
time: 955 us; the launch traced here: 951 us
  waiting for transfers between devices  504 us (53%)
  other arithmetic  244 us (26%)
  matrix products  132 us (14%)
  local copies, waits for them, and re-layouts  29.1 us (3%)
  between operations  20.1 us (2%)
  blocking collectives  14.1 us (1%)
    psum x1, waiting for transfers between devices, body(): first_image = lax.psum(partial_image, 'fsdp')  123 us
    psum x1, waiting for transfers between devices, body(): second_gram = lax.psum(gram_local(second), 'fsdp')  107 us
    reduce_scatter x1, waiting for transfers between devices, body(): lax.psum_scatter(jnp.dot(all_hidden, down_weight, preferred_element_type=...  94.5 us
    another operation x15, other arithmetic, body(): jnp.linalg.cholesky(second_gram)  79.5 us
    another operation x5, other arithmetic, solve_rows(): jax.scipy.linalg.solve_triangular(lower_factor, image_rows.T, lower=True)  79.3 us
    another operation x14, other arithmetic, body(): first_factor = jnp.linalg.cholesky(first_gram)  78.5 us
    all_to_all x1, waiting for transfers between devices, body(): lax.all_to_all(jnp.stack([mlp_out * marked[:, None]] * lax.axis_size('fsd...  50.6 us
    psum x1, waiting for transfers between devices, body(): second = lax.psum(partial_second, 'tensor')  45.6 us
  transfers between devices with their start and end apart: 7, of which 7 were waited for; matrix products, arithmetic and copies ran while one was open for 0% of the time, Pallas kernels for 0%

profile of v1, /device:TPU:1, one launch (start us, length us, event | category | flops | bytes accessed | tf_op | source)
XLA Modules:
  0.0 951.2 jit_solution(8934179416089410934)
XLA Ops:
  7.2 14.1 %all_gather.3 = bf16[512,896]{1,0:T(8,128)(2,1)S(1)} all-gather(bf16[128,896]{1,0:T(8,128)(2,1)} %param.6), channel_id=1, replica_groups=mesh['fsdp'=32,'tensor'=4] {'tensor'}, dimensions={0}, use_global_device_ids=true | all-gather | bytes 1146880 | tf_op jit(solution)/shard_map/all_gather | solution.py:37
  31.8 94.5 %reduce-scatter.2.cloned.1.call-done = f32[16,4096]{1,0:T(8,128)} async-done(((f32[512,4096]{1,0:T(8,128)}), f32[16,4096]{1,0:T(8,128)}) %reduce-scatter.2.cloned.1.call-update) | async-done | bytes 262160 | tf_op jit(solution)/shard_map/reduce_scatter | solution.py:38
  138.0 50.6 %all-to-all-done = bf16[32,16,4096]{2,1,0:T(8,128)(2,1)} async-done(((bf16[32,16,4096]{2,1,0:T(8,128)(2,1)}), bf16[32,16,4096]{2,1,0:T(8,128)(2,1)}, u32[]{:S(2)}, u32[]{:S(2)}) %all-to-all-start) | async-done | bytes 4194336 | tf_op jit(solution)/shard_map/all_to_all | solution.py:51
  190.8 40.2 %all-reduce.7.cloned.1.call-done = bf16[512,512]{1,0:T(8,128)(2,1)} async-done(((bf16[512,512]{1,0:T(8,128)(2,1)}), bf16[512,512]{1,0:T(8,128)(2,1)}) %all-reduce.7.cloned.1.call-update) | async-done | bytes 524304 | tf_op jit(solution)/shard_map/psum | solution.py:13
  241.9 15.7 %fusion.97 = f32[4096,512]{1,0:T(8,128)} fusion(f32[4096,512]{1,0:T(8,128)S(1)} %multiply_add_fusion, f32[512,512]{1,0:T(8,128)S(1)} %copy-done), kind=kOutput, calls=%fused_computation.170 | convolution fusion | flops 12884901888 | bytes 17825792 | tf_op jit(solution)/shard_map/dot_general | solution.py:63
  258.1 122.6 %all-reduce.9.cloned.1.call-done = f32[4096,512]{1,0:T(8,128)} async-done(((f32[4096,512]{1,0:T(8,128)}), f32[4096,512]{1,0:T(8,128)}) %all-reduce.9.cloned.1.call-update) | async-done | bytes 8388624 | tf_op jit(solution)/shard_map/psum | solution.py:66
  380.7 18.5 %fusion.98 = f32[512,512]{0,1:T(8,128)} fusion(f32[4096,512]{1,0:T(8,128)} %all-reduce.9.cloned.1.call-done), kind=kOutput, calls=%fused_computation.171 | convolution fusion | flops 12884901888 | bytes 9437184 | tf_op jit(solution)/shard_map/dot_general | solution.py:17
  400.3 43.1 %all-reduce.11.cloned.1.call-done = f32[512,512]{0,1:T(8,128)} async-done(((f32[512,512]{0,1:T(8,128)}), f32[512,512]{0,1:T(8,128)}) %all-reduce.11.cloned.1.call-update) | async-done | bytes 1048592 | tf_op jit(solution)/shard_map/psum | solution.py:67
  446.4 11.7 %cholesky.286 = f32[128,128]{1,0:T(8,128)S(1)} custom-call(f32[128,128]{1,0:T(8,128)S(1)} %cholesky.426), custom_call_target="Cholesky" | custom-call | tf_op jit(solution)/shard_map/jit(cholesky)/cholesky | solution.py:69
  468.8 11.7 %cholesky.305 = f32[128,128]{1,0:T(8,128)S(1)} custom-call(f32[128,128]{1,0:T(8,128)S(1)} %cholesky.430), custom_call_target="Cholesky" | custom-call | tf_op jit(solution)/shard_map/jit(cholesky)/cholesky | solution.py:69
  480.5 10.0 %custom-call.37 = f32[1,128,128]{1,2,0:T(8,128)S(1)} custom-call(f32[1,128,128]{2,1,0:T(8,128)S(1)} %get-tuple-element.67), custom_call_target="InvertDiagBlocksLowerTriangular" | custom-call | tf_op jit(solution)/shard_map/jit(cholesky)/cholesky | solution.py:69
  491.1 11.7 %cholesky.326 = f32[128,128]{1,0:T(8,128)S(1)} custom-call(f32[128,128]{1,0:T(8,128)S(1)} %cholesky.435), custom_call_target="Cholesky" | custom-call | tf_op jit(solution)/shard_map/jit(cholesky)/cholesky | solution.py:69
  513.3 11.7 %cholesky.343 = f32[128,128]{1,0:T(8,128)S(1)} custom-call(f32[128,128]{1,0:T(8,128)S(1)} %convolution_subtract_fusion.13), custom_call_target="Cholesky" | custom-call | tf_op jit(solution)/shard_map/jit(cholesky)/cholesky | solution.py:69
  537.7 39.3 %custom-call.31 = f32[4,128,128]{1,2,0:T(8,128)S(1)} custom-call(f32[4,128,128]{2,1,0:T(8,128)S(1)} %get-tuple-element.12), custom_call_target="InvertDiagBlocksLowerTriangular" | custom-call | tf_op jit(solution)/shard_map/jit(_solve_triangular)/triangular_solve | solution.py:26
  598.5 12.4 %fusion.14 = f32[128,4096]{0,1:T(8,128)S(1)} fusion(f32[128,4096]{1,0:T(8,128)S(1)} %fusion.80, f32[128,4096]{1,0:T(8,128)S(1)} %fusion.78, f32[128,4096]{1,0:T(8,128)S(1)} %fusion.20, f32[512,4096]{0,1:T(8,128)} %bitcast.128, f32[512,512]{1,0:T(8,128)S(1)} %get-tuple-element.179), kind=kOutput, calls=%fused_computation.21 | convolution fusion | flops 2419589120 | bytes 10682368 | tf_op jit(solution)/shard_map/jit(_solve_triangular)/triangular_solve | solution.py:26
  612.9 29.5 %fusion = f32[512,512]{1,0:T(8,128)} fusion(f32[4096,512]{1,0:T(8,128)S(1)} %bitcast.130, f32[128,4096]{1,0:T(8,128)S(1)} %fusion.82, f32[128,4096]{1,0:T(8,128)S(1)} %fusion.80, f32[128,4096]{1,0:T(8,128)S(1)} %fusion.78, f32[128,4096]{1,0:T(8,128)S(1)} %fusion.20), kind=kOutput, calls=%fused_computation.4 | convolution fusion | flops 12891193344 | bytes 17825792 | tf_op jit(solution)/shard_map/dot_general | solution.py:72
  644.0 45.6 %all-reduce.13.cloned.1.call-done = f32[512,512]{1,0:T(8,128)} async-done(((f32[512,512]{1,0:T(8,128)}), f32[512,512]{1,0:T(8,128)}) %all-reduce.13.cloned.1.call-update) | async-done | bytes 1048592 | tf_op jit(solution)/shard_map/psum | solution.py:79
  695.7 106.8 %all-reduce.15.cloned.1.call-done = f32[512,512]{0,1:T(8,128)} async-done(((f32[512,512]{0,1:T(8,128)}), f32[512,512]{0,1:T(8,128)}) %all-reduce.15.cloned.1.call-update) | async-done | bytes 1048592 | tf_op jit(solution)/shard_map/psum | solution.py:80
  805.5 11.7 %cholesky.358 = f32[128,128]{1,0:T(8,128)S(1)} custom-call(f32[128,128]{1,0:T(8,128)S(1)} %cholesky.439), custom_call_target="Cholesky" | custom-call | tf_op jit(solution)/shard_map/jit(cholesky)/cholesky | solution.py:81
  827.9 11.9 %cholesky.377 = f32[128,128]{1,0:T(8,128)S(1)} custom-call(f32[128,128]{1,0:T(8,128)S(1)} %cholesky.443), custom_call_target="Cholesky" | custom-call | tf_op jit(solution)/shard_map/jit(cholesky)/cholesky | solution.py:81
  839.8 9.8 %custom-call.40 = f32[1,128,128]{1,2,0:T(8,128)S(1)} custom-call(f32[1,128,128]{2,1,0:T(8,128)S(1)} %get-tuple-element.57), custom_call_target="InvertDiagBlocksLowerTriangular" | custom-call | tf_op jit(solution)/shard_map/jit(cholesky)/cholesky | solution.py:81
  850.3 11.7 %cholesky.398 = f32[128,128]{1,0:T(8,128)S(1)} custom-call(f32[128,128]{1,0:T(8,128)S(1)} %cholesky.448), custom_call_target="Cholesky" | custom-call | tf_op jit(solution)/shard_map/jit(cholesky)/cholesky | solution.py:81
  872.5 11.9 %cholesky.415 = f32[128,128]{1,0:T(8,128)S(1)} custom-call(f32[128,128]{1,0:T(8,128)S(1)} %convolution_subtract_fusion.11), custom_call_target="Cholesky" | custom-call | tf_op jit(solution)/shard_map/jit(cholesky)/cholesky | solution.py:81
  898.3 39.3 %custom-call.32 = f32[4,128,128]{1,2,0:T(8,128)S(1)} custom-call(f32[4,128,128]{2,1,0:T(8,128)S(1)} %get-tuple-element.20), custom_call_target="InvertDiagBlocksLowerTriangular" | custom-call | tf_op jit(solution)/shard_map/jit(_solve_triangular)/triangular_solve | solution.py:26
  (136 shorter events, 160.9 us)
Async XLA Ops:
  7.2 234.7 %copy-start = (f32[512,512]{1,0:T(8,128)S(1)}, f32[512,512]{1,0:T(8,128)}, u32[]{:S(2)}) copy-start(f32[512,512]{1,0:T(8,128)} %param.10) | copy-start | bytes 3145732
  7.2 119.2 %reduce-scatter.2.cloned.1.call-start = ((), (), s32[]{:S(2)}) async-start(), calls=%async_computation.2 | async-start | bytes 8650752 | tf_op jit(solution)/shard_map/reduce_scatter | solution.py:38
  31.1 0.7 copy-start.4
  130.5 58.1 %all-to-all-start = ((bf16[32,16,4096]{2,1,0:T(8,128)(2,1)}), bf16[32,16,4096]{2,1,0:T(8,128)(2,1)}, u32[]{:S(2)}, u32[]{:S(2)}) async-start(bf16[32,16,4096]{2,1,0:T(8,128)(2,1)} %stack.2), calls=%async_computation.1 | async-start | bytes 8388608 | tf_op jit(solution)/shard_map/all_to_all | solution.py:51
  138.0 93.1 %all-reduce.7.cloned.1.call-start = ((), (), s32[]{:S(2)}) async-start(), calls=%async_computation.3 | async-start | bytes 1048576 | tf_op jit(solution)/shard_map/psum | solution.py:13
  190.6 190.1 %all-reduce.9.cloned.1.call-start = ((), (), s32[]{:S(2)}) async-start(), calls=%async_computation.4 | async-start | bytes 16777216 | tf_op jit(solution)/shard_map/psum | solution.py:66
  238.5 3.4 copy-start.2
  257.6 185.8 %all-reduce.11.cloned.1.call-start = ((), (), s32[]{:S(2)}) async-start(), calls=%async_computation.5 | async-start | bytes 2097152 | tf_op jit(solution)/shard_map/psum | solution.py:67
  399.2 290.4 %all-reduce.13.cloned.1.call-start = ((), (), s32[]{:S(2)}) async-start(), calls=%async_computation.6 | async-start | bytes 2097152 | tf_op jit(solution)/shard_map/psum | solution.py:79
  596.5 16.4 %slice-start = ((s8[8388608]{0:T(1024)(128)(4,1)}), s8[4194304]{0:T(1024)(128)(4,1)S(1)}, s32[]{:S(2)}) async-start(s8[8388608]{0:T(1024)(128)(4,1)} %bitcast.129), calls=%async_computation.8 | async-start | bytes 8388608
  598.5 14.4 %slice-start.1 = ((s8[8388608]{0:T(1024)(128)(4,1)}), s8[4194304]{0:T(1024)(128)(4,1)S(1)}, s32[]{:S(2)}) async-start(s8[8388608]{0:T(1024)(128)(4,1)} %bitcast.129), calls=%async_computation.9 | async-start | bytes 8388608
  642.4 160.1 %all-reduce.15.cloned.1.call-start = ((), (), s32[]{:S(2)}) async-start(), calls=%async_computation.7 | async-start | bytes 2097152 | tf_op jit(solution)/shard_map/psum | solution.py:80
  805.5 132.1 %copy-start.3 = (f32[512,512]{1,0:T(8,128)S(1)}, f32[512,512]{1,0:T(8,128)}, u32[]{:S(2)}) copy-start(f32[512,512]{1,0:T(8,128)} %all-reduce.13.cloned.1.call-done) | copy-start | bytes 3145732
  938.1 5.8 copy-start.1
Sparse Core Ops, SparseCore 0:
  31.2 95.0 reduce-scatter.1
  190.7 40.2 all-reduce.6
  257.7 122.9 all-reduce.8
  399.4 43.9 all-reduce.10
  642.6 47.0 all-reduce.12
  694.1 108.3 all-reduce.14
